TPU v7x, 32 devices: a whole 2x2x4 slice. The times are simulated.
32 devices in a mesh: lsec: 4 (over y, x), rsec: 8 (over z, core).
Axes of the slice: x: 2, y: 2, z: 4, core: 2. Of those that a mesh axis runs over, the one named last changes fastest.
Arguments:
- psi: bfloat16 [16, 16, 256, 256], P('lsec', 'rsec'), may hold values from -6 to 6
- left_env: bfloat16 [16, 4, 256, 256], P('lsec'), may hold values from -0.375 to 0.375
- right_env: bfloat16 [16, 4, 256, 256], P('rsec'), may hold values from -0.1875 to 0.1875
- energies: float32 [16, 16], P('lsec', 'rsec'), may hold values from 0.5 to 3
- coef_num: int32 [2], replicated, may hold values from 3 to 9
- coef_den: int32 [2], replicated, may hold values from 4 to 8
Outputs:
- vector_out: bfloat16 [16, 16, 256, 256], P('lsec', 'rsec')
- ritz: float32 [3], replicated
All inputs are finite; a program needn't handle non-finite values.
Results may differ from a plain program's by a relative error of at most 0.015.
Values may be sent and summed in bfloat16 or wider, within the bound.
A program may use at most 64 MiB of HBM per device.

v0:
```python
import jax
import jax.numpy as jnp
from jax import lax
from jax.sharding import PartitionSpec as P

DIAG = 2
HOPS = 1
ITERS = 3
eps = 1e-06


def padded(block, sides, width):
    for axis, dim in sides:
        count = lax.axis_size(axis)
        forward = [(i, i + 1) for i in range(count - 1)]
        backward = [(target, source) for source, target in forward]
        low = lax.ppermute(
            lax.slice_in_dim(block, block.shape[dim] - width, None, axis=dim), axis, forward
        )
        high = lax.ppermute(lax.slice_in_dim(block, 0, width, axis=dim), axis, backward)
        block = jnp.concatenate([low, block, high], axis=dim)
    return block


def add_terms(left_env, right_env, source, first, number, total):
    for term in range(first, first + number):
        inner = jnp.einsum(
            "aij,abjk->abik", left_env[:, term], source, preferred_element_type=jnp.float32
        ).astype(jnp.bfloat16)
        total = total + jnp.einsum(
            "abik,blk->abil", inner, right_env[:, term], preferred_element_type=jnp.float32
        )
    return total


def with_rims(vec):
    wide = padded(vec, (("rsec", 1),), 1)
    full = padded(wide, (("lsec", 0),), 1)
    return full


def matvec(vec, left_env, right_env, energies):
    vals = vec.astype(jnp.float32)
    total = energies[:, :, None, None] * vals
    total = add_terms(left_env, right_env, vec, 0, DIAG, total)
    full = with_rims(vec)
    plus_blocks = full[:-2, 2:]
    minus_blocks = full[2:, :-2]
    total = add_terms(left_env, right_env, plus_blocks, DIAG, HOPS, total)
    total = add_terms(left_env, right_env, minus_blocks, DIAG + HOPS, HOPS, total)
    return total


def per_device(psi, left_env, right_env, energies, coef_num, coef_den):
    count = 1.0 / float(psi.size * lax.axis_size("lsec") * lax.axis_size("rsec"))
    start_vals = psi.astype(jnp.float32)
    start = lax.psum(jnp.sum(start_vals * start_vals), ("lsec", "rsec")) * count
    vec = (start_vals * lax.rsqrt(start + eps)).astype(jnp.bfloat16)
    previous = jnp.zeros(psi.shape, jnp.float32)
    thetas = []
    for step in range(ITERS):
        sigma = matvec(vec, left_env, right_env, energies)
        vals = vec.astype(jnp.float32)
        if step == 0:
            coef = jnp.float32(0.0)
        else:
            coef = coef_num[step - 1].astype(jnp.float32) / coef_den[step - 1].astype(jnp.float32)
        sums = lax.psum(
            (
                jnp.sum(sigma * sigma),
                jnp.sum(sigma * vals),
                jnp.sum(sigma * previous),
                jnp.sum(vals * vals),
                jnp.sum(vals * previous),
                jnp.sum(previous * previous),
            ),
            ("lsec", "rsec"),
        )
        m_ss, m_sv, m_sp, m_vv, m_vp, m_pp = [part * count for part in sums]
        resid = sigma - m_sv * vals - coef * previous
        norm_sq = (
            m_ss
            - 2.0 * m_sv * m_sv
            - 2.0 * coef * m_sp
            + m_sv * m_sv * m_vv
            + 2.0 * m_sv * coef * m_vp
            + coef * coef * m_pp
        )
        thetas.append(m_sv)
        previous = vals
        vec = (resid * lax.rsqrt(norm_sq + eps)).astype(jnp.bfloat16)
    return (vec, jnp.stack(thetas))


def solution(mesh):
    in_specs = (
        P("lsec", "rsec", None, None),
        P("lsec", None, None, None),
        P("rsec", None, None, None),
        P("lsec", "rsec"),
        P(),
        P(),
    )
    out_specs = (P("lsec", "rsec", None, None), P())
    return jax.shard_map(
        per_device, mesh=mesh, in_specs=in_specs, out_specs=out_specs, check_vma=False
    )
```

profile of v0, /device:TPU:0, one launch (start us, length us, event | category | flops | bytes accessed | tf_op | source)
XLA Modules:
  0.0 343.5 jit_solution(12554492794385849762)
XLA Ops:
  0.6 2.4 fusion
  3.0 42.2 %psum.125 = f32[]{:T(128)} all-reduce(f32[]{:T(128)} %fusion), channel_id=1, replica_groups=mesh['lsec'=4,'rsec'=8] {'lsec','rsec'}, use_global_device_ids=true, to_apply=%region_1.0 | all-reduce | flops 1 | bytes 8 | tf_op jit(solution)/shard_map/psum | solution.py:57
  47.4 1.5 collective-permute-start
  50.3 4.0 %collective-permute-done.1 = bf16[4,1,256,256]{3,2,0,1:T(8,128)(2,1)S(1)} collective-permute-done((bf16[4,1,256,256]{3,2,0,1:T(8,128)(2,1)S(1)}, bf16[4,1,256,256]{3,2,0,1:T(8,128)(2,1)S(1)}, u32[]{:S(2)}, u32[]{:S(2)}) %collective-permute-start.1) | collective-permute-done | bytes 524320 | tf_op jit(solution)/shard_map/ppermute | solution.py:20
  55.5 5.0 %collective-permute-start.2 = (bf16[1,4,256,256]{3,2,0,1:T(8,128)(2,1)}, bf16[1,4,256,256]{3,2,0,1:T(8,128)(2,1)}, u32[]{:S(2)}, u32[]{:S(2)}) collective-permute-start(bf16[1,4,256,256]{3,2,0,1:T(8,128)(2,1)} %get-tuple-element.40), channel_id=1, source_target_pairs={{0,8},{8,16},{16,24},{1,9},{9,17},{17,25},{2,10},{10,18},{18,26},{... | collective-permute-start | bytes 1572872 | tf_op jit(solution)/shard_map/ppermute | solution.py:17
  60.5 3.0 fusion.37
  64.7 3.0 fusion.39
  67.8 3.2 fusion.41
  71.0 9.3 %collective-permute-done.3 = bf16[1,4,256,256]{3,2,0,1:T(8,128)(2,1)} collective-permute-done((bf16[1,4,256,256]{3,2,0,1:T(8,128)(2,1)}, bf16[1,4,256,256]{3,2,0,1:T(8,128)(2,1)}, u32[]{:S(2)}, u32[]{:S(2)}) %collective-permute-start.3) | collective-permute-done | bytes 524320 | tf_op jit(solution)/shard_map/ppermute | solution.py:20
  80.3 6.9 %multiply_reduce_fusion.2 = (f32[]{:T(128)}, f32[]{:T(128)}, f32[]{:T(128)}, f32[]{:T(128)}, f32[]{:T(128)}, /*index=5*/f32[4,2,256,256]{3,2,0,1:T(8,128)}) fusion(bf16[4,2,256,256]{3,2,0,1:T(8,128)(2,1)S(1)} %fusion.1, bf16[2,4,256,256]{3,2,1,0:T(8,128)(2,1)} %param.8, bf16[1,4,256,256]{3,2,0,1:T(8,128)(2,1)} %collective-permute-done.3, ...), kind=kOutput, calls=%fused_computation.59 | convolution fusion | flops 549978112 | bytes 12846100 | tf_op jit(solution)/shard_map/abik,blk->abil/dot_general | solution.py:30
  87.2 50.7 %all-reduce.2 = (f32[]{:T(128)}, f32[]{:T(128)}, f32[]{:T(128)}, f32[]{:T(128)}, f32[]{:T(128)}, /*index=5*/f32[]{:T(128)}) all-reduce(f32[]{:T(128)} %get-tuple-element.13, f32[]{:T(128)} %get-tuple-element.14, f32[]{:T(128)} %get-tuple-element.12, f32[]{:T(128)} %get-tuple-element.16, ...), channel_id=1, replica_groups=mesh['lsec'=4,'rsec'=8] {'lsec','rsec'}, use_global_device_ids=true, to_apply=%region_5.0 | all-reduce | flops 6 | bytes 48 | tf_op jit(solution)/shard_map/psum | solution.py:68
  143.8 2.0 fusion.19
  146.9 2.1 collective-permute-start.4
  153.5 2.2 pad_maximum_fusion.57
  155.6 5.0 %collective-permute-start.6 = (bf16[1,4,256,256]{3,2,0,1:T(8,128)(2,1)}, bf16[1,4,256,256]{3,2,0,1:T(8,128)(2,1)}, u32[]{:S(2)}, u32[]{:S(2)}) collective-permute-start(bf16[1,4,256,256]{3,2,0,1:T(8,128)(2,1)} %get-tuple-element.38), channel_id=1, source_target_pairs={{0,8},{8,16},{16,24},{1,9},{9,17},{17,25},{2,10},{10,18},{18,26},{... | collective-permute-start | bytes 1572872 | tf_op jit(solution)/shard_map/ppermute | solution.py:17
  160.6 3.1 fusion.44
  165.0 3.2 fusion.46
  168.2 3.3 fusion.48
  171.6 9.2 %collective-permute-done.7 = bf16[1,4,256,256]{3,2,0,1:T(8,128)(2,1)} collective-permute-done((bf16[1,4,256,256]{3,2,0,1:T(8,128)(2,1)}, bf16[1,4,256,256]{3,2,0,1:T(8,128)(2,1)}, u32[]{:S(2)}, u32[]{:S(2)}) %collective-permute-start.7) | collective-permute-done | bytes 524320 | tf_op jit(solution)/shard_map/ppermute | solution.py:20
  180.7 7.0 %fusion.25 = (f32[]{:T(128)}, f32[]{:T(128)}, f32[]{:T(128)}, f32[]{:T(128)}, f32[]{:T(128)}, /*index=5*/f32[4,2,256,256]{3,2,0,1:T(8,128)}) fusion(bf16[4,2,256,256]{3,2,0,1:T(8,128)(2,1)S(1)} %fusion.1, bf16[4,2,256,256]{3,2,0,1:T(8,128)(2,1)S(1)} %fusion.19, bf16[2,4,256,256]{3,2,1,0:T(8,128)(2,1)} %param.8, ...), kind=kOutput, calls=%fused_computation.46 | convolution fusion | flops 550502400 | bytes 13894676 | tf_op jit(solution)/shard_map/abik,blk->abil/dot_general | solution.py:30
  187.8 48.5 %all-reduce.1 = (f32[]{:T(128)}, f32[]{:T(128)}, f32[]{:T(128)}, f32[]{:T(128)}, f32[]{:T(128)}) all-reduce(f32[]{:T(128)} %get-tuple-element.9, f32[]{:T(128)} %get-tuple-element.10, f32[]{:T(128)} %get-tuple-element.8, f32[]{:T(128)} %get-tuple-element.17, f32[]{:T(128)} %get-tuple-element.11), channel_id=1, replica_groups=mesh['lsec'=4,'rsec'=8] {'lsec','rsec'}, use_global_device_ids=true, to_apply=%region_16.0 | all-reduce | flops 5 | bytes 40 | tf_op jit(solution)/shard_map/psum | solution.py:68
  241.2 2.2 fusion.24
  244.4 2.2 collective-permute-start.8
  250.8 2.2 pad_maximum_fusion.54
  253.0 5.0 %collective-permute-start.10 = (bf16[1,4,256,256]{3,2,0,1:T(8,128)(2,1)}, bf16[1,4,256,256]{3,2,0,1:T(8,128)(2,1)}, u32[]{:S(2)}, u32[]{:S(2)}) collective-permute-start(bf16[1,4,256,256]{3,2,0,1:T(8,128)(2,1)} %get-tuple-element.36), channel_id=1, source_target_pairs={{0,8},{8,16},{16,24},{1,9},{9,17},{17,25},{2,10},{10,18},{18,26},{... | collective-permute-start | bytes 1572872 | tf_op jit(solution)/shard_map/ppermute | solution.py:17
  257.9 3.0 fusion.51
  262.3 3.1 fusion.53
  265.4 3.3 fusion.55
  268.7 9.3 %collective-permute-done.11 = bf16[1,4,256,256]{3,2,0,1:T(8,128)(2,1)} collective-permute-done((bf16[1,4,256,256]{3,2,0,1:T(8,128)(2,1)}, bf16[1,4,256,256]{3,2,0,1:T(8,128)(2,1)}, u32[]{:S(2)}, u32[]{:S(2)}) %collective-permute-start.11) | collective-permute-done | bytes 524320 | tf_op jit(solution)/shard_map/ppermute | solution.py:20
  278.0 6.9 %fusion.34 = (f32[]{:T(128)}, f32[]{:T(128)}, f32[]{:T(128)}, f32[]{:T(128)}, f32[]{:T(128)}, /*index=5*/f32[4,2,256,256]{3,2,0,1:T(8,128)}) fusion(bf16[4,2,256,256]{3,2,0,1:T(8,128)(2,1)S(1)} %fusion.19, bf16[4,2,256,256]{3,2,0,1:T(8,128)(2,1)S(1)} %fusion.24, bf16[2,4,256,256]{3,2,1,0:T(8,128)(2,1)S(1)} %copy-done.2, ...), kind=kOutput, calls=%fused_computation.55 | convolution fusion | flops 550502400 | bytes 13894676 | tf_op jit(solution)/shard_map/abik,blk->abil/dot_general | solution.py:30
  284.9 49.4 %all-reduce = (f32[]{:T(128)}, f32[]{:T(128)}, f32[]{:T(128)}, f32[]{:T(128)}, f32[]{:T(128)}) all-reduce(f32[]{:T(128)} %get-tuple-element.5, f32[]{:T(128)} %get-tuple-element.6, f32[]{:T(128)} %get-tuple-element.4, f32[]{:T(128)} %get-tuple-element.18, f32[]{:T(128)} %get-tuple-element.7), channel_id=1, replica_groups=mesh['lsec'=4,'rsec'=8] {'lsec','rsec'}, use_global_device_ids=true, to_apply=%region_26.0 | all-reduce | flops 5 | bytes 40 | tf_op jit(solution)/shard_map/psum | solution.py:68
  339.7 2.1 fusion.10
  (39 shorter events, 16.3 us)
Async XLA Ops:
  47.4 13.1 %copy-start.1 = (bf16[4,4,256,256]{3,2,1,0:T(8,128)(2,1)S(1)}, bf16[4,4,256,256]{3,2,1,0:T(8,128)(2,1)}, u32[]{:S(2)}) copy-start(bf16[4,4,256,256]{3,2,1,0:T(8,128)(2,1)} %param.7) | copy-start | bytes 6291460
  47.4 2.9 collective-permute-start
  48.8 5.5 %collective-permute-start.1 = (bf16[4,1,256,256]{3,2,0,1:T(8,128)(2,1)S(1)}, bf16[4,1,256,256]{3,2,0,1:T(8,128)(2,1)S(1)}, u32[]{:S(2)}, u32[]{:S(2)}) collective-permute-start(bf16[4,1,256,256]{3,2,0,1:T(8,128)(2,1)S(1)} %get-tuple-element.46), channel_id=1, source_target_pairs={{1,0},{2,1},{3,2},{4,3},{5,4},{6,5},{7,6},{9,8},{10,9},{11,10},{12... | collective-permute-start | bytes 1572872 | tf_op jit(solution)/shard_map/ppermute | solution.py:20
  50.3 4.0 %copy-start.3 = (bf16[4,1,256,256]{3,2,0,1:T(8,128)(2,1)}, bf16[4,1,256,256]{3,2,0,1:T(8,128)(2,1)S(1)}, u32[]{:S(2)}) copy-start(bf16[4,1,256,256]{3,2,0,1:T(8,128)(2,1)S(1)} %collective-permute-done) | copy-start | bytes 1572868
  54.3 1.1 copy-start.4
  55.5 12.3 %collective-permute-start.2 = (bf16[1,4,256,256]{3,2,0,1:T(8,128)(2,1)}, bf16[1,4,256,256]{3,2,0,1:T(8,128)(2,1)}, u32[]{:S(2)}, u32[]{:S(2)}) collective-permute-start(bf16[1,4,256,256]{3,2,0,1:T(8,128)(2,1)} %get-tuple-element.40), channel_id=1, source_target_pairs={{0,8},{8,16},{16,24},{1,9},{9,17},{17,25},{2,10},{10,18},{18,26},{... | collective-permute-start | bytes 1572872 | tf_op jit(solution)/shard_map/ppermute | solution.py:17
  63.4 16.8 %collective-permute-start.3 = (bf16[1,4,256,256]{3,2,0,1:T(8,128)(2,1)}, bf16[1,4,256,256]{3,2,0,1:T(8,128)(2,1)}, u32[]{:S(2)}, u32[]{:S(2)}) collective-permute-start(bf16[1,4,256,256]{3,2,0,1:T(8,128)(2,1)} %get-tuple-element.39), channel_id=1, source_target_pairs={{8,0},{16,8},{24,16},{9,1},{17,9},{25,17},{10,2},{18,10},{26,18},{... | collective-permute-start | bytes 1572872 | tf_op jit(solution)/shard_map/ppermute | solution.py:20
  67.7 12.5 %copy-start.7 = (f32[4,2]{0,1:T(2,128)S(1)}, f32[4,2]{0,1:T(2,128)}, u32[]{:S(2)}) copy-start(f32[4,2]{0,1:T(2,128)} %param.9) | copy-start | bytes 100
  71.0 72.9 %copy-start = (bf16[4,2,256,256]{3,2,1,0:T(8,128)(2,1)S(1)}, bf16[4,2,256,256]{3,2,1,0:T(8,128)(2,1)}, u32[]{:S(2)}) copy-start(bf16[4,2,256,256]{3,2,1,0:T(8,128)(2,1)} %param.6) | copy-start | bytes 3145732
  145.8 4.5 %copy-start.5 = (s32[2]{0:T(128)S(1)}, s32[2]{0:T(128)}, u32[]{:S(2)}) copy-start(s32[2]{0:T(128)} %param.10) | copy-start | bytes 28
  145.8 5.7 %copy-start.6 = (s32[2]{0:T(128)S(1)}, s32[2]{0:T(128)}, u32[]{:S(2)}) copy-start(s32[2]{0:T(128)} %param.11) | copy-start | bytes 28
  146.9 6.6 %collective-permute-start.4 = (bf16[4,1,256,256]{3,2,0,1:T(8,128)(2,1)}, bf16[4,1,256,256]{3,2,0,1:T(8,128)(2,1)}, u32[]{:S(2)}, u32[]{:S(2)}) collective-permute-start(bf16[4,1,256,256]{3,2,0,1:T(8,128)(2,1)} %get-tuple-element.43), channel_id=1, source_target_pairs={{0,1},{1,2},{2,3},{3,4},{4,5},{5,6},{6,7},{8,9},{9,10},{10,11},{11... | collective-permute-start | bytes 1572872 | tf_op jit(solution)/shard_map/ppermute | solution.py:17
  149.0 4.5 %collective-permute-start.5 = (bf16[4,1,256,256]{3,2,0,1:T(8,128)(2,1)}, bf16[4,1,256,256]{3,2,0,1:T(8,128)(2,1)}, u32[]{:S(2)}, u32[]{:S(2)}) collective-permute-start(bf16[4,1,256,256]{3,2,0,1:T(8,128)(2,1)} %get-tuple-element.44), channel_id=1, source_target_pairs={{1,0},{2,1},{3,2},{4,3},{5,4},{6,5},{7,6},{9,8},{10,9},{11,10},{12... | collective-permute-start | bytes 1572872 | tf_op jit(solution)/shard_map/ppermute | solution.py:20
  155.6 12.6 %collective-permute-start.6 = (bf16[1,4,256,256]{3,2,0,1:T(8,128)(2,1)}, bf16[1,4,256,256]{3,2,0,1:T(8,128)(2,1)}, u32[]{:S(2)}, u32[]{:S(2)}) collective-permute-start(bf16[1,4,256,256]{3,2,0,1:T(8,128)(2,1)} %get-tuple-element.38), channel_id=1, source_target_pairs={{0,8},{8,16},{16,24},{1,9},{9,17},{17,25},{2,10},{10,18},{18,26},{... | collective-permute-start | bytes 1572872 | tf_op jit(solution)/shard_map/ppermute | solution.py:17
  163.8 17.0 %collective-permute-start.7 = (bf16[1,4,256,256]{3,2,0,1:T(8,128)(2,1)}, bf16[1,4,256,256]{3,2,0,1:T(8,128)(2,1)}, u32[]{:S(2)}, u32[]{:S(2)}) collective-permute-start(bf16[1,4,256,256]{3,2,0,1:T(8,128)(2,1)} %get-tuple-element.37), channel_id=1, source_target_pairs={{8,0},{16,8},{24,16},{9,1},{17,9},{25,17},{10,2},{18,10},{26,18},{... | collective-permute-start | bytes 1572872 | tf_op jit(solution)/shard_map/ppermute | solution.py:20
  244.4 13.5 %copy-start.2 = (bf16[2,4,256,256]{3,2,1,0:T(8,128)(2,1)S(1)}, bf16[2,4,256,256]{3,2,1,0:T(8,128)(2,1)}, u32[]{:S(2)}) copy-start(bf16[2,4,256,256]{3,2,1,0:T(8,128)(2,1)} %param.8) | copy-start | bytes 3145732
  244.4 5.5 %collective-permute-start.8 = (bf16[4,1,256,256]{3,2,0,1:T(8,128)(2,1)}, bf16[4,1,256,256]{3,2,0,1:T(8,128)(2,1)}, u32[]{:S(2)}, u32[]{:S(2)}) collective-permute-start(bf16[4,1,256,256]{3,2,0,1:T(8,128)(2,1)} %get-tuple-element.41), channel_id=1, source_target_pairs={{0,1},{1,2},{2,3},{3,4},{4,5},{5,6},{6,7},{8,9},{9,10},{10,11},{11... | collective-permute-start | bytes 1572872 | tf_op jit(solution)/shard_map/ppermute | solution.py:17
  246.6 4.1 %collective-permute-start.9 = (bf16[4,1,256,256]{3,2,0,1:T(8,128)(2,1)}, bf16[4,1,256,256]{3,2,0,1:T(8,128)(2,1)}, u32[]{:S(2)}, u32[]{:S(2)}) collective-permute-start(bf16[4,1,256,256]{3,2,0,1:T(8,128)(2,1)} %get-tuple-element.42), channel_id=1, source_target_pairs={{1,0},{2,1},{3,2},{4,3},{5,4},{6,5},{7,6},{9,8},{10,9},{11,10},{12... | collective-permute-start | bytes 1572872 | tf_op jit(solution)/shard_map/ppermute | solution.py:20
  253.0 12.4 %collective-permute-start.10 = (bf16[1,4,256,256]{3,2,0,1:T(8,128)(2,1)}, bf16[1,4,256,256]{3,2,0,1:T(8,128)(2,1)}, u32[]{:S(2)}, u32[]{:S(2)}) collective-permute-start(bf16[1,4,256,256]{3,2,0,1:T(8,128)(2,1)} %get-tuple-element.36), channel_id=1, source_target_pairs={{0,8},{8,16},{16,24},{1,9},{9,17},{17,25},{2,10},{10,18},{18,26},{... | collective-permute-start | bytes 1572872 | tf_op jit(solution)/shard_map/ppermute | solution.py:17
  261.0 17.0 %collective-permute-start.11 = (bf16[1,4,256,256]{3,2,0,1:T(8,128)(2,1)}, bf16[1,4,256,256]{3,2,0,1:T(8,128)(2,1)}, u32[]{:S(2)}, u32[]{:S(2)}) collective-permute-start(bf16[1,4,256,256]{3,2,0,1:T(8,128)(2,1)} %get-tuple-element.35), channel_id=1, source_target_pairs={{8,0},{16,8},{24,16},{9,1},{17,9},{25,17},{10,2},{18,10},{26,18},{... | collective-permute-start | bytes 1572872 | tf_op jit(solution)/shard_map/ppermute | solution.py:20
where the time goes:
time: 345 us; the launch traced here: 343 us
  blocking collectives  191 us (55%)
  matrix products  49.2 us (14%)
  waiting for transfers between devices  32.9 us (10%)
  starting transfers between devices  28.5 us (8%)
  between operations  21.7 us (6%)
  other arithmetic  16.1 us (5%)
  local copies, waits for them, and re-layouts  4.39 us (1%)
    psum x3, blocking collectives, per_device(): lax.psum((jnp.sum(sigma * sigma), jnp.sum(sigma * vals), jnp.sum(sigma *...  149 us
    dot_general x12, matrix products, add_terms(): jnp.einsum('abik,blk->abil', inner, right_env[:, term], preferred_element...  49.2 us
    psum x1, blocking collectives, per_device(): start = lax.psum(jnp.sum(start_vals * start_vals), ('lsec', 'rsec')) * count  42.2 us
    ppermute x6, waiting for transfers between devices, padded(): lax.ppermute(lax.slice_in_dim(block, 0, width, axis=dim), axis, backward)  32.7 us
    ppermute x6, starting transfers between devices, padded(): lax.ppermute(lax.slice_in_dim(block, block.shape[dim] - width, None, axis...  20.8 us
    ppermute x6, starting transfers between devices, padded(): lax.ppermute(lax.slice_in_dim(block, 0, width, axis=dim), axis, backward)  7.69 us
  transfers between devices with their start and end apart: 12, of which 6 were waited for; matrix products, arithmetic and copies ran while one was open for 9% of the time, Pallas kernels for 0%

commit v1 on v0

--- a/solution.py
+++ b/solution.py
@@ -66,15 +66,18 @@
         else:
             coef = coef_num[step - 1].astype(jnp.float32) / coef_den[step - 1].astype(jnp.float32)
         sums = lax.psum(
-            (
-                jnp.sum(sigma * sigma),
-                jnp.sum(sigma * vals),
-                jnp.sum(sigma * previous),
-                jnp.sum(vals * vals),
-                jnp.sum(vals * previous),
-                jnp.sum(previous * previous),
+            lax.psum(
+                (
+                    jnp.sum(sigma * sigma),
+                    jnp.sum(sigma * vals),
+                    jnp.sum(sigma * previous),
+                    jnp.sum(vals * vals),
+                    jnp.sum(vals * previous),
+                    jnp.sum(previous * previous),
+                ),
+                "rsec",
             ),
-            ("lsec", "rsec"),
+            "lsec",
         )
         m_ss, m_sv, m_sp, m_vv, m_vp, m_pp = [part * count for part in sums]
         resid = sigma - m_sv * vals - coef * previous

time: 345 us -> 289 us (0.84)
  blocking collectives: 191 us -> 136 us
    psum x3, blocking collectives: 149 us -> 67.8 us  [per_device(): lax.psum((jnp.sum(sigma * sigma), jnp.sum(sigma * vals), jnp.sum(sigma *...]
    psum x0 -> x3, blocking collectives: none -> 26.2 us  [per_device(): lax.psum(lax.psum((jnp.sum(sigma * sigma), jnp.sum(sigma * vals), jnp.sum...]
  transfers between devices with their start and end apart: 12 -> 12, of which waited for: 6 -> 6; matrix products, arithmetic and copies ran while one was open for 9% -> 10% of each run, Pallas kernels for 0% -> 0%
where the time goes in v1:
time: 289 us; the launch traced here: 288 us
  blocking collectives  136 us (47%)
  matrix products  49.2 us (17%)
  waiting for transfers between devices  33.7 us (12%)
  starting transfers between devices  26.7 us (9%)
  between operations  21.6 us (7%)
  other arithmetic  16.1 us (6%)
  local copies, waits for them, and re-layouts  4.39 us (2%)
    psum x3, blocking collectives, per_device(): lax.psum((jnp.sum(sigma * sigma), jnp.sum(sigma * vals), jnp.sum(sigma *...  67.8 us
    dot_general x12, matrix products, add_terms(): jnp.einsum('abik,blk->abil', inner, right_env[:, term], preferred_element...  49.2 us
    psum x1, blocking collectives, per_device(): start = lax.psum(jnp.sum(start_vals * start_vals), ('lsec', 'rsec')) * count  42.2 us
    ppermute x6, waiting for transfers between devices, padded(): lax.ppermute(lax.slice_in_dim(block, 0, width, axis=dim), axis, backward)  33.5 us
    psum x3, blocking collectives, per_device(): lax.psum(lax.psum((jnp.sum(sigma * sigma), jnp.sum(sigma * vals), jnp.sum...  26.2 us
    ppermute x6, starting transfers between devices, padded(): lax.ppermute(lax.slice_in_dim(block, block.shape[dim] - width, None, axis...  19 us
    ppermute x6, starting transfers between devices, padded(): lax.ppermute(lax.slice_in_dim(block, 0, width, axis=dim), axis, backward)  7.69 us
    convert_element_type x3, other arithmetic, per_device(): vec = (resid * lax.rsqrt(norm_sq + eps)).astype(jnp.bfloat16)  6.25 us
  transfers between devices with their start and end apart: 12, of which 6 were waited for; matrix products, arithmetic and copies ran while one was open for 10% of the time, Pallas kernels for 0%

profile of v1, /device:TPU:0, one launch (start us, length us, event | category | flops | bytes accessed | tf_op | source)
XLA Modules:
  0.0 287.8 jit_solution(6876270962718620609)
XLA Ops:
  0.6 2.4 fusion
  3.0 42.2 %psum.243 = f32[]{:T(128)} all-reduce(f32[]{:T(128)} %fusion), channel_id=1, replica_groups=mesh['lsec'=4,'rsec'=8] {'lsec','rsec'}, use_global_device_ids=true, to_apply=%region_1.0 | all-reduce | flops 1 | bytes 8 | tf_op jit(solution)/shard_map/psum | solution.py:57
  50.3 4.0 %collective-permute-done.1 = bf16[4,1,256,256]{3,2,0,1:T(8,128)(2,1)S(1)} collective-permute-done((bf16[4,1,256,256]{3,2,0,1:T(8,128)(2,1)S(1)}, bf16[4,1,256,256]{3,2,0,1:T(8,128)(2,1)S(1)}, u32[]{:S(2)}, u32[]{:S(2)}) %collective-permute-start.1) | collective-permute-done | bytes 524320 | tf_op jit(solution)/shard_map/ppermute | solution.py:20
  55.5 5.0 %collective-permute-start.2 = (bf16[1,4,256,256]{3,2,0,1:T(8,128)(2,1)}, bf16[1,4,256,256]{3,2,0,1:T(8,128)(2,1)}, u32[]{:S(2)}, u32[]{:S(2)}) collective-permute-start(bf16[1,4,256,256]{3,2,0,1:T(8,128)(2,1)} %get-tuple-element.56), channel_id=1, source_target_pairs={{0,8},{8,16},{16,24},{1,9},{9,17},{17,25},{2,10},{10,18},{18,26},{... | collective-permute-start | bytes 1572872 | tf_op jit(solution)/shard_map/ppermute | solution.py:17
  60.5 3.0 %fusion.37 = f32[2,4,256,256]{3,2,1,0:T(8,128)} fusion(bf16[4,2,256,256]{3,2,0,1:T(8,128)(2,1)S(1)} %fusion.1, bf16[4,4,256,256]{3,2,1,0:T(8,128)(2,1)S(1)} %copy-done.1, bf16[2,4,256,256]{3,2,1,0:T(8,128)(2,1)} %param.8), kind=kOutput, calls=%fused_computation.74 | convolution fusion | flops 537395200 | bytes 3932160 | tf_op jit(solution)/shard_map/abik,blk->abil/dot_general | solution.py:30
  64.7 3.0 %fusion.39 = f32[2,4,256,256]{3,2,1,0:T(8,128)} fusion(bf16[4,2,256,256]{3,2,0,1:T(8,128)(2,1)S(1)} %fusion.1, bf16[4,4,256,256]{3,2,1,0:T(8,128)(2,1)S(1)} %copy-done.1, bf16[2,4,256,256]{3,2,1,0:T(8,128)(2,1)} %param.8), kind=kOutput, calls=%fused_computation.76 | convolution fusion | flops 537395200 | bytes 3932160 | tf_op jit(solution)/shard_map/abik,blk->abil/dot_general | solution.py:30
  67.7 3.2 %fusion.41 = f32[2,4,256,256]{3,2,1,0:T(8,128)} fusion(bf16[1,4,256,256]{3,2,0,1:T(8,128)(2,1)} %collective-permute-done.2, bf16[4,1,256,256]{3,2,0,1:T(8,128)(2,1)} %copy-done.4, bf16[4,2,256,256]{3,2,0,1:T(8,128)(2,1)S(1)} %fusion.1, bf16[4,1,256,256]{3,2,0,1:T(8,128)(2,1)} %copy-done.3, bf16[4,4,256,256]{3,2,1,0:T(8,128)(2,1)S(1)} %copy-done.1, ...), kind=kOutput, calls=%fused_computation.78 | convolution fusion | flops 541589504 | bytes 5505024 | tf_op jit(solution)/shard_map/abik,blk->abil/dot_general | solution.py:30
  70.9 9.3 %collective-permute-done.3 = bf16[1,4,256,256]{3,2,0,1:T(8,128)(2,1)} collective-permute-done((bf16[1,4,256,256]{3,2,0,1:T(8,128)(2,1)}, bf16[1,4,256,256]{3,2,0,1:T(8,128)(2,1)}, u32[]{:S(2)}, u32[]{:S(2)}) %collective-permute-start.3) | collective-permute-done | bytes 524320 | tf_op jit(solution)/shard_map/ppermute | solution.py:20
  80.2 6.9 %multiply_reduce_fusion.2 = (f32[]{:T(128)}, f32[]{:T(128)}, f32[]{:T(128)}, f32[]{:T(128)}, f32[]{:T(128)}, /*index=5*/f32[4,2,256,256]{3,2,0,1:T(8,128)}) fusion(bf16[4,2,256,256]{3,2,0,1:T(8,128)(2,1)S(1)} %fusion.1, bf16[2,4,256,256]{3,2,1,0:T(8,128)(2,1)} %param.8, bf16[1,4,256,256]{3,2,0,1:T(8,128)(2,1)} %collective-permute-done.3, ...), kind=kOutput, calls=%fused_computation.59 | convolution fusion | flops 549978112 | bytes 12846100 | tf_op jit(solution)/shard_map/abik,blk->abil/dot_general | solution.py:30
  87.2 24.5 %all-reduce.2 = (f32[]{:T(128)}, f32[]{:T(128)}, f32[]{:T(128)}, f32[]{:T(128)}, f32[]{:T(128)}, /*index=5*/f32[]{:T(128)}) all-reduce(f32[]{:T(128)} %get-tuple-element.13, f32[]{:T(128)} %get-tuple-element.14, f32[]{:T(128)} %get-tuple-element.12, f32[]{:T(128)} %get-tuple-element.16, ...), channel_id=1, replica_groups=mesh['lsec'=4,'rsec'=8] {'rsec'}, use_global_device_ids=true, to_apply=%region_6.0 | all-reduce | flops 6 | bytes 48 | tf_op jit(solution)/shard_map/psum | solution.py:69
  111.7 8.7 %all-reduce.5 = (f32[]{:T(128)}, f32[]{:T(128)}, f32[]{:T(128)}, f32[]{:T(128)}, f32[]{:T(128)}, /*index=5*/f32[]{:T(128)}) all-reduce(f32[]{:T(128)} %get-tuple-element.29, f32[]{:T(128)} %get-tuple-element.30, f32[]{:T(128)} %get-tuple-element.31, f32[]{:T(128)} %get-tuple-element.32, ...), channel_id=1, replica_groups=mesh['lsec'=4,'rsec'=8] {'lsec'}, use_global_device_ids=true, to_apply=%region_7.0 | all-reduce | flops 6 | bytes 48 | tf_op jit(solution)/shard_map/psum | solution.py:68
  129.1 2.1 collective-permute-start.4
  135.7 2.2 pad_maximum_fusion.57
  137.9 4.1 %collective-permute-start.6 = (bf16[1,4,256,256]{3,2,0,1:T(8,128)(2,1)}, bf16[1,4,256,256]{3,2,0,1:T(8,128)(2,1)}, u32[]{:S(2)}, u32[]{:S(2)}) collective-permute-start(bf16[1,4,256,256]{3,2,0,1:T(8,128)(2,1)} %get-tuple-element.54), channel_id=1, source_target_pairs={{0,8},{8,16},{16,24},{1,9},{9,17},{17,25},{2,10},{10,18},{18,26},{... | collective-permute-start | bytes 1572872 | tf_op jit(solution)/shard_map/ppermute | solution.py:17
  142.0 3.1 %fusion.44 = f32[2,4,256,256]{3,2,1,0:T(8,128)} fusion(bf16[4,2,256,256]{3,2,0,1:T(8,128)(2,1)S(1)} %fusion.19, bf16[4,4,256,256]{3,2,1,0:T(8,128)(2,1)} %param.7, bf16[2,4,256,256]{3,2,1,0:T(8,128)(2,1)} %param.8), kind=kOutput, calls=%fused_computation.81 | convolution fusion | flops 537395200 | bytes 3932160 | tf_op jit(solution)/shard_map/abik,blk->abil/dot_general | solution.py:30
  146.4 3.2 %fusion.46 = f32[2,4,256,256]{3,2,1,0:T(8,128)} fusion(bf16[4,2,256,256]{3,2,0,1:T(8,128)(2,1)S(1)} %fusion.19, bf16[4,4,256,256]{3,2,1,0:T(8,128)(2,1)} %param.7, bf16[2,4,256,256]{3,2,1,0:T(8,128)(2,1)} %param.8), kind=kOutput, calls=%fused_computation.83 | convolution fusion | flops 537395200 | bytes 3932160 | tf_op jit(solution)/shard_map/abik,blk->abil/dot_general | solution.py:30
  149.6 3.4 %fusion.48 = f32[2,4,256,256]{3,2,1,0:T(8,128)} fusion(bf16[1,4,256,256]{3,2,0,1:T(8,128)(2,1)} %collective-permute-done.6, bf16[4,1,256,256]{3,2,0,1:T(8,128)(2,1)} %collective-permute-done.5, bf16[4,2,256,256]{3,2,0,1:T(8,128)(2,1)S(1)} %fusion.19, bf16[4,1,256,256]{3,2,0,1:T(8,128)(2,1)} %collective-permute-done.4, bf16[4,4,256,256]{3,2,1,0:T(8,128)(2,1)} %param.7, ...), kind=kOutput, calls=%fused_computation.85 | convolution fusion | flops 541589504 | bytes 5505024 | tf_op jit(solution)/shard_map/abik,blk->abil/dot_general | solution.py:30
  153.0 9.7 %collective-permute-done.7 = bf16[1,4,256,256]{3,2,0,1:T(8,128)(2,1)} collective-permute-done((bf16[1,4,256,256]{3,2,0,1:T(8,128)(2,1)}, bf16[1,4,256,256]{3,2,0,1:T(8,128)(2,1)}, u32[]{:S(2)}, u32[]{:S(2)}) %collective-permute-start.7) | collective-permute-done | bytes 524320 | tf_op jit(solution)/shard_map/ppermute | solution.py:20
  162.7 7.0 %fusion.25 = (f32[]{:T(128)}, f32[]{:T(128)}, f32[]{:T(128)}, f32[]{:T(128)}, f32[]{:T(128)}, /*index=5*/f32[4,2,256,256]{3,2,0,1:T(8,128)}) fusion(bf16[4,2,256,256]{3,2,0,1:T(8,128)(2,1)S(1)} %fusion.1, bf16[4,2,256,256]{3,2,0,1:T(8,128)(2,1)S(1)} %fusion.19, bf16[2,4,256,256]{3,2,1,0:T(8,128)(2,1)} %param.8, ...), kind=kOutput, calls=%fused_computation.46 | convolution fusion | flops 550502400 | bytes 13894676 | tf_op jit(solution)/shard_map/abik,blk->abil/dot_general | solution.py:30
  169.7 21.3 %all-reduce.1 = (f32[]{:T(128)}, f32[]{:T(128)}, f32[]{:T(128)}, f32[]{:T(128)}, f32[]{:T(128)}) all-reduce(f32[]{:T(128)} %get-tuple-element.9, f32[]{:T(128)} %get-tuple-element.10, f32[]{:T(128)} %get-tuple-element.8, f32[]{:T(128)} %get-tuple-element.17, f32[]{:T(128)} %get-tuple-element.11), channel_id=1, replica_groups=mesh['lsec'=4,'rsec'=8] {'rsec'}, use_global_device_ids=true, to_apply=%region_23.0 | all-reduce | flops 5 | bytes 40 | tf_op jit(solution)/shard_map/psum | solution.py:69
  191.0 8.7 %all-reduce.4 = (f32[]{:T(128)}, f32[]{:T(128)}, f32[]{:T(128)}, f32[]{:T(128)}, f32[]{:T(128)}) all-reduce(f32[]{:T(128)} %get-tuple-element.24, f32[]{:T(128)} %get-tuple-element.25, f32[]{:T(128)} %get-tuple-element.26, f32[]{:T(128)} %get-tuple-element.27, f32[]{:T(128)} %get-tuple-element.28), channel_id=1, replica_groups=mesh['lsec'=4,'rsec'=8] {'lsec'}, use_global_device_ids=true, to_apply=%region_24.0 | all-reduce | flops 5 | bytes 40 | tf_op jit(solution)/shard_map/psum | solution.py:68
  205.0 2.2 fusion.24
  208.2 2.2 collective-permute-start.8
  214.6 2.2 pad_maximum_fusion.54
  216.7 4.1 %collective-permute-start.10 = (bf16[1,4,256,256]{3,2,0,1:T(8,128)(2,1)}, bf16[1,4,256,256]{3,2,0,1:T(8,128)(2,1)}, u32[]{:S(2)}, u32[]{:S(2)}) collective-permute-start(bf16[1,4,256,256]{3,2,0,1:T(8,128)(2,1)} %get-tuple-element.52), channel_id=1, source_target_pairs={{0,8},{8,16},{16,24},{1,9},{9,17},{17,25},{2,10},{10,18},{18,26},{... | collective-permute-start | bytes 1572872 | tf_op jit(solution)/shard_map/ppermute | solution.py:17
  220.9 3.0 %fusion.51 = f32[2,4,256,256]{3,2,1,0:T(8,128)} fusion(bf16[4,2,256,256]{3,2,0,1:T(8,128)(2,1)S(1)} %fusion.24, bf16[4,4,256,256]{3,2,1,0:T(8,128)(2,1)} %param.7, bf16[2,4,256,256]{3,2,1,0:T(8,128)(2,1)S(1)} %copy-done.2), kind=kOutput, calls=%fused_computation.88 | convolution fusion | flops 537395200 | bytes 3932160 | tf_op jit(solution)/shard_map/abik,blk->abil/dot_general | solution.py:30
  225.2 3.1 %fusion.53 = f32[2,4,256,256]{3,2,1,0:T(8,128)} fusion(bf16[4,2,256,256]{3,2,0,1:T(8,128)(2,1)S(1)} %fusion.24, bf16[4,4,256,256]{3,2,1,0:T(8,128)(2,1)} %param.7, bf16[2,4,256,256]{3,2,1,0:T(8,128)(2,1)S(1)} %copy-done.2), kind=kOutput, calls=%fused_computation.90 | convolution fusion | flops 537395200 | bytes 3932160 | tf_op jit(solution)/shard_map/abik,blk->abil/dot_general | solution.py:30
  228.3 3.3 %fusion.55 = f32[2,4,256,256]{3,2,1,0:T(8,128)} fusion(bf16[1,4,256,256]{3,2,0,1:T(8,128)(2,1)} %collective-permute-done.10, bf16[4,1,256,256]{3,2,0,1:T(8,128)(2,1)} %collective-permute-done.9, bf16[4,2,256,256]{3,2,0,1:T(8,128)(2,1)S(1)} %fusion.24, bf16[4,1,256,256]{3,2,0,1:T(8,128)(2,1)} %collective-permute-done.8, bf16[4,4,256,256]{3,2,1,0:T(8,128)(2,1)} %param.7, ...), kind=kOutput, calls=%fused_computation.92 | convolution fusion | flops 541589504 | bytes 5505024 | tf_op jit(solution)/shard_map/abik,blk->abil/dot_general | solution.py:30
  231.6 9.5 %collective-permute-done.11 = bf16[1,4,256,256]{3,2,0,1:T(8,128)(2,1)} collective-permute-done((bf16[1,4,256,256]{3,2,0,1:T(8,128)(2,1)}, bf16[1,4,256,256]{3,2,0,1:T(8,128)(2,1)}, u32[]{:S(2)}, u32[]{:S(2)}) %collective-permute-start.11) | collective-permute-done | bytes 524320 | tf_op jit(solution)/shard_map/ppermute | solution.py:20
  241.1 6.9 %fusion.34 = (f32[]{:T(128)}, f32[]{:T(128)}, f32[]{:T(128)}, f32[]{:T(128)}, f32[]{:T(128)}, /*index=5*/f32[4,2,256,256]{3,2,0,1:T(8,128)}) fusion(bf16[4,2,256,256]{3,2,0,1:T(8,128)(2,1)S(1)} %fusion.19, bf16[4,2,256,256]{3,2,0,1:T(8,128)(2,1)S(1)} %fusion.24, bf16[2,4,256,256]{3,2,1,0:T(8,128)(2,1)S(1)} %copy-done.2, ...), kind=kOutput, calls=%fused_computation.55 | convolution fusion | flops 550502400 | bytes 13894676 | tf_op jit(solution)/shard_map/abik,blk->abil/dot_general | solution.py:30
  248.1 22.0 %all-reduce = (f32[]{:T(128)}, f32[]{:T(128)}, f32[]{:T(128)}, f32[]{:T(128)}, f32[]{:T(128)}) all-reduce(f32[]{:T(128)} %get-tuple-element.5, f32[]{:T(128)} %get-tuple-element.6, f32[]{:T(128)} %get-tuple-element.4, f32[]{:T(128)} %get-tuple-element.18, f32[]{:T(128)} %get-tuple-element.7), channel_id=1, replica_groups=mesh['lsec'=4,'rsec'=8] {'rsec'}, use_global_device_ids=true, to_apply=%region_38.0 | all-reduce | flops 5 | bytes 40 | tf_op jit(solution)/shard_map/psum | solution.py:69
  270.1 8.7 %all-reduce.3 = (f32[]{:T(128)}, f32[]{:T(128)}, f32[]{:T(128)}, f32[]{:T(128)}, f32[]{:T(128)}) all-reduce(f32[]{:T(128)} %get-tuple-element.19, f32[]{:T(128)} %get-tuple-element.20, f32[]{:T(128)} %get-tuple-element.21, f32[]{:T(128)} %get-tuple-element.22, f32[]{:T(128)} %get-tuple-element.23), channel_id=1, replica_groups=mesh['lsec'=4,'rsec'=8] {'lsec'}, use_global_device_ids=true, to_apply=%region_39.0 | all-reduce | flops 5 | bytes 40 | tf_op jit(solution)/shard_map/psum | solution.py:68
  (42 shorter events, 21.9 us)
Async XLA Ops:
  47.4 13.1 %copy-start.1 = (bf16[4,4,256,256]{3,2,1,0:T(8,128)(2,1)S(1)}, bf16[4,4,256,256]{3,2,1,0:T(8,128)(2,1)}, u32[]{:S(2)}) copy-start(bf16[4,4,256,256]{3,2,1,0:T(8,128)(2,1)} %param.7) | copy-start | bytes 6291460
  47.4 2.9 %collective-permute-start = (bf16[4,1,256,256]{3,2,0,1:T(8,128)(2,1)S(1)}, bf16[4,1,256,256]{3,2,0,1:T(8,128)(2,1)S(1)}, u32[]{:S(2)}, u32[]{:S(2)}) collective-permute-start(bf16[4,1,256,256]{3,2,0,1:T(8,128)(2,1)S(1)} %get-tuple-element.61), channel_id=1, source_target_pairs={{0,1},{1,2},{2,3},{3,4},{4,5},{5,6},{6,7},{8,9},{9,10},{10,11},{11... | collective-permute-start | bytes 1572872 | tf_op jit(solution)/shard_map/ppermute | solution.py:17
  48.8 5.5 %collective-permute-start.1 = (bf16[4,1,256,256]{3,2,0,1:T(8,128)(2,1)S(1)}, bf16[4,1,256,256]{3,2,0,1:T(8,128)(2,1)S(1)}, u32[]{:S(2)}, u32[]{:S(2)}) collective-permute-start(bf16[4,1,256,256]{3,2,0,1:T(8,128)(2,1)S(1)} %get-tuple-element.62), channel_id=1, source_target_pairs={{1,0},{2,1},{3,2},{4,3},{5,4},{6,5},{7,6},{9,8},{10,9},{11,10},{12... | collective-permute-start | bytes 1572872 | tf_op jit(solution)/shard_map/ppermute | solution.py:20
  50.3 4.0 %copy-start.3 = (bf16[4,1,256,256]{3,2,0,1:T(8,128)(2,1)}, bf16[4,1,256,256]{3,2,0,1:T(8,128)(2,1)S(1)}, u32[]{:S(2)}) copy-start(bf16[4,1,256,256]{3,2,0,1:T(8,128)(2,1)S(1)} %collective-permute-done) | copy-start | bytes 1572868
  54.3 1.1 copy-start.4
  55.5 12.3 %collective-permute-start.2 = (bf16[1,4,256,256]{3,2,0,1:T(8,128)(2,1)}, bf16[1,4,256,256]{3,2,0,1:T(8,128)(2,1)}, u32[]{:S(2)}, u32[]{:S(2)}) collective-permute-start(bf16[1,4,256,256]{3,2,0,1:T(8,128)(2,1)} %get-tuple-element.56), channel_id=1, source_target_pairs={{0,8},{8,16},{16,24},{1,9},{9,17},{17,25},{2,10},{10,18},{18,26},{... | collective-permute-start | bytes 1572872 | tf_op jit(solution)/shard_map/ppermute | solution.py:17
  63.4 16.8 %collective-permute-start.3 = (bf16[1,4,256,256]{3,2,0,1:T(8,128)(2,1)}, bf16[1,4,256,256]{3,2,0,1:T(8,128)(2,1)}, u32[]{:S(2)}, u32[]{:S(2)}) collective-permute-start(bf16[1,4,256,256]{3,2,0,1:T(8,128)(2,1)} %get-tuple-element.55), channel_id=1, source_target_pairs={{8,0},{16,8},{24,16},{9,1},{17,9},{25,17},{10,2},{18,10},{26,18},{... | collective-permute-start | bytes 1572872 | tf_op jit(solution)/shard_map/ppermute | solution.py:20
  67.7 12.5 %copy-start.7 = (f32[4,2]{0,1:T(2,128)S(1)}, f32[4,2]{0,1:T(2,128)}, u32[]{:S(2)}) copy-start(f32[4,2]{0,1:T(2,128)} %param.9) | copy-start | bytes 100
  70.9 55.1 %copy-start = (bf16[4,2,256,256]{3,2,1,0:T(8,128)(2,1)S(1)}, bf16[4,2,256,256]{3,2,1,0:T(8,128)(2,1)}, u32[]{:S(2)}) copy-start(bf16[4,2,256,256]{3,2,1,0:T(8,128)(2,1)} %param.6) | copy-start | bytes 3145732
  128.1 4.5 %copy-start.5 = (s32[2]{0:T(128)S(1)}, s32[2]{0:T(128)}, u32[]{:S(2)}) copy-start(s32[2]{0:T(128)} %param.10) | copy-start | bytes 28
  128.1 5.7 %copy-start.6 = (s32[2]{0:T(128)S(1)}, s32[2]{0:T(128)}, u32[]{:S(2)}) copy-start(s32[2]{0:T(128)} %param.11) | copy-start | bytes 28
  129.1 6.6 %collective-permute-start.4 = (bf16[4,1,256,256]{3,2,0,1:T(8,128)(2,1)}, bf16[4,1,256,256]{3,2,0,1:T(8,128)(2,1)}, u32[]{:S(2)}, u32[]{:S(2)}) collective-permute-start(bf16[4,1,256,256]{3,2,0,1:T(8,128)(2,1)} %get-tuple-element.59), channel_id=1, source_target_pairs={{0,1},{1,2},{2,3},{3,4},{4,5},{5,6},{6,7},{8,9},{9,10},{10,11},{11... | collective-permute-start | bytes 1572872 | tf_op jit(solution)/shard_map/ppermute | solution.py:17
  131.2 4.5 %collective-permute-start.5 = (bf16[4,1,256,256]{3,2,0,1:T(8,128)(2,1)}, bf16[4,1,256,256]{3,2,0,1:T(8,128)(2,1)}, u32[]{:S(2)}, u32[]{:S(2)}) collective-permute-start(bf16[4,1,256,256]{3,2,0,1:T(8,128)(2,1)} %get-tuple-element.60), channel_id=1, source_target_pairs={{1,0},{2,1},{3,2},{4,3},{5,4},{6,5},{7,6},{9,8},{10,9},{11,10},{12... | collective-permute-start | bytes 1572872 | tf_op jit(solution)/shard_map/ppermute | solution.py:20
  137.9 11.7 %collective-permute-start.6 = (bf16[1,4,256,256]{3,2,0,1:T(8,128)(2,1)}, bf16[1,4,256,256]{3,2,0,1:T(8,128)(2,1)}, u32[]{:S(2)}, u32[]{:S(2)}) collective-permute-start(bf16[1,4,256,256]{3,2,0,1:T(8,128)(2,1)} %get-tuple-element.54), channel_id=1, source_target_pairs={{0,8},{8,16},{16,24},{1,9},{9,17},{17,25},{2,10},{10,18},{18,26},{... | collective-permute-start | bytes 1572872 | tf_op jit(solution)/shard_map/ppermute | solution.py:17
  145.1 17.5 %collective-permute-start.7 = (bf16[1,4,256,256]{3,2,0,1:T(8,128)(2,1)}, bf16[1,4,256,256]{3,2,0,1:T(8,128)(2,1)}, u32[]{:S(2)}, u32[]{:S(2)}) collective-permute-start(bf16[1,4,256,256]{3,2,0,1:T(8,128)(2,1)} %get-tuple-element.53), channel_id=1, source_target_pairs={{8,0},{16,8},{24,16},{9,1},{17,9},{25,17},{10,2},{18,10},{26,18},{... | collective-permute-start | bytes 1572872 | tf_op jit(solution)/shard_map/ppermute | solution.py:20
  208.2 12.7 %copy-start.2 = (bf16[2,4,256,256]{3,2,1,0:T(8,128)(2,1)S(1)}, bf16[2,4,256,256]{3,2,1,0:T(8,128)(2,1)}, u32[]{:S(2)}) copy-start(bf16[2,4,256,256]{3,2,1,0:T(8,128)(2,1)} %param.8) | copy-start | bytes 3145732
  208.2 5.5 %collective-permute-start.8 = (bf16[4,1,256,256]{3,2,0,1:T(8,128)(2,1)}, bf16[4,1,256,256]{3,2,0,1:T(8,128)(2,1)}, u32[]{:S(2)}, u32[]{:S(2)}) collective-permute-start(bf16[4,1,256,256]{3,2,0,1:T(8,128)(2,1)} %get-tuple-element.57), channel_id=1, source_target_pairs={{0,1},{1,2},{2,3},{3,4},{4,5},{5,6},{6,7},{8,9},{9,10},{10,11},{11... | collective-permute-start | bytes 1572872 | tf_op jit(solution)/shard_map/ppermute | solution.py:17
  210.4 4.1 %collective-permute-start.9 = (bf16[4,1,256,256]{3,2,0,1:T(8,128)(2,1)}, bf16[4,1,256,256]{3,2,0,1:T(8,128)(2,1)}, u32[]{:S(2)}, u32[]{:S(2)}) collective-permute-start(bf16[4,1,256,256]{3,2,0,1:T(8,128)(2,1)} %get-tuple-element.58), channel_id=1, source_target_pairs={{1,0},{2,1},{3,2},{4,3},{5,4},{6,5},{7,6},{9,8},{10,9},{11,10},{12... | collective-permute-start | bytes 1572872 | tf_op jit(solution)/shard_map/ppermute | solution.py:20
  216.7 11.6 %collective-permute-start.10 = (bf16[1,4,256,256]{3,2,0,1:T(8,128)(2,1)}, bf16[1,4,256,256]{3,2,0,1:T(8,128)(2,1)}, u32[]{:S(2)}, u32[]{:S(2)}) collective-permute-start(bf16[1,4,256,256]{3,2,0,1:T(8,128)(2,1)} %get-tuple-element.52), channel_id=1, source_target_pairs={{0,8},{8,16},{16,24},{1,9},{9,17},{17,25},{2,10},{10,18},{18,26},{... | collective-permute-start | bytes 1572872 | tf_op jit(solution)/shard_map/ppermute | solution.py:17
  223.9 17.2 %collective-permute-start.11 = (bf16[1,4,256,256]{3,2,0,1:T(8,128)(2,1)}, bf16[1,4,256,256]{3,2,0,1:T(8,128)(2,1)}, u32[]{:S(2)}, u32[]{:S(2)}) collective-permute-start(bf16[1,4,256,256]{3,2,0,1:T(8,128)(2,1)} %get-tuple-element.51), channel_id=1, source_target_pairs={{8,0},{16,8},{24,16},{9,1},{17,9},{25,17},{10,2},{18,10},{26,18},{... | collective-permute-start | bytes 1572872 | tf_op jit(solution)/shard_map/ppermute | solution.py:20
